TPU v7x, 512 devices: a whole 4x4x16 slice. The times are simulated.
512 devices in a mesh: chan: 32 (over y, z_lo), ctx: 16 (over z_hi, x, core).
Axes of the slice: x: 4, y: 4, z: 16 (z_hi: 2, z_lo: 8; z = z_hi * 8 + z_lo), core: 2. Of those that a mesh axis runs over, the one named last changes fastest.
Arguments:
- inputs: bfloat16 [2048, 8192], P('ctx', 'chan'), may hold values from -6 to 6
- gate: bfloat16 [2048, 8192], P('ctx', 'chan'), may hold values from -200 to 200
- filter_taps: bfloat16 [2048, 8192], P('ctx', 'chan'), may hold values from -4 to 4, as said below
- cotangent: bfloat16 [2048, 8192], P('ctx', 'chan'), may hold values from -6 to 6
Outputs:
- output: bfloat16 [2048, 8192], P('ctx', 'chan')
- gate_grad: bfloat16 [2048, 8192], P('ctx', 'chan')
- input_grad: bfloat16 [2048, 8192], P('ctx', 'chan')
- filter_grad: float32 [2048, 8192], P('ctx', 'chan')
Inputs may be any that keep to these rules, and one draw needn't show every extreme that they name: `filter_taps`: each channel's filter taps shrink with the lag at a rate of their own.
All inputs are finite; a program needn't handle non-finite values.
Results may differ from a plain program's by a relative error of at most 0.005.
Values may be sent and summed in bfloat16 or wider, within the bound.
A program may use at most 64 MiB of HBM per device.

v0:
```python
import math
import jax
import jax.numpy as jnp
from jax import lax
from jax.sharding import PartitionSpec as P

HIGHEST = lax.Precision.HIGHEST
EPSILON = 1e-06


def tables(block_len):
    period = 2 * block_len
    offsets = jnp.arange(block_len, dtype=jnp.int32)
    harmonics = jnp.arange(block_len + 1, dtype=jnp.int32)
    samples = jnp.arange(period, dtype=jnp.int32)
    radians = math.pi / block_len
    angles = jnp.mod(harmonics[:, None] * offsets[None, :], period).astype(jnp.float32) * radians
    back_angles = (
        jnp.mod(samples[:, None] * harmonics[None, :], period).astype(jnp.float32) * radians
    )
    weights = (
        jnp.where((harmonics == 0) | (harmonics == block_len), 1.0, 2.0).astype(jnp.float32)
        / period
    )
    return (
        jnp.cos(angles),
        jnp.sin(angles),
        jnp.cos(back_angles) * weights[None, :],
        jnp.sin(back_angles) * weights[None, :],
    )


def spectrum(series, block_len, fwd_cos, fwd_sin):
    number = series.shape[0] // block_len
    blocks = series.astype(jnp.float32).reshape(number, block_len, series.shape[1])
    real_part = jnp.einsum("kn,bnc->bkc", fwd_cos, blocks, precision=HIGHEST)
    imag_part = -jnp.einsum("kn,bnc->bkc", fwd_sin, blocks, precision=HIGHEST)
    return (real_part, imag_part)


def inverse_many(real_part, imag_part, inv_cos, inv_sin):
    return jnp.einsum("mk,skc->smc", inv_cos, real_part, precision=HIGHEST) - jnp.einsum(
        "mk,skc->smc", inv_sin, imag_part, precision=HIGHEST
    )


def select(spectra, position):
    number = spectra[0].shape[0]
    inside = jnp.logical_and(position >= 0, position < number)
    clipped = jnp.clip(position, 0, number - 1)
    real_part = lax.dynamic_index_in_dim(spectra[0], clipped, 0, keepdims=False)
    imag_part = lax.dynamic_index_in_dim(spectra[1], clipped, 0, keepdims=False)
    return (jnp.where(inside, real_part, 0.0), jnp.where(inside, imag_part, 0.0))


def product(left, right, conjugate):
    if conjugate:
        return (left[0] * right[0] + left[1] * right[1], left[0] * right[1] - left[1] * right[0])
    return (left[0] * right[0] - left[1] * right[1], left[0] * right[1] + left[1] * right[0])


def forward_terms(taps_spec, input_spec, first_block, targets):
    empty = jnp.zeros((targets,) + taps_spec[0].shape[1:], jnp.float32)

    def forward_advance(offset, totals):
        reals, imags = totals
        kernel = select(taps_spec, offset)
        for target in range(targets):
            addend = product(kernel, select(input_spec, first_block - 1 + target - offset), False)
            reals = reals.at[target].add(addend[0])
            imags = imags.at[target].add(addend[1])
        return (reals, imags)

    return lax.fori_loop(0, taps_spec[0].shape[0], forward_advance, (empty, empty))


def backward_terms(taps_spec, inner_spec, first_block, targets):
    empty = jnp.zeros((targets,) + taps_spec[0].shape[1:], jnp.float32)

    def backward_advance(offset, totals):
        reals, imags = totals
        kernel = select(taps_spec, offset)
        for target in range(targets):
            addend = product(kernel, select(inner_spec, first_block + target + offset), True)
            reals = reals.at[target].add(addend[0])
            imags = imags.at[target].add(addend[1])
        return (reals, imags)

    return lax.fori_loop(0, taps_spec[0].shape[0], backward_advance, (empty, empty))


def owner_terms(input_spec, inner_spec, first_block, targets):
    empty = jnp.zeros((targets,) + input_spec[0].shape[1:], jnp.float32)

    def owner_advance(later, totals):
        reals, imags = totals
        grads = select(inner_spec, later)
        for target in range(targets):
            addend = product(select(input_spec, later - first_block - target), grads, True)
            reals = reals.at[target].add(addend[0])
            imags = imags.at[target].add(addend[1])
        return (reals, imags)

    return lax.fori_loop(0, input_spec[0].shape[0], owner_advance, (empty, empty))


def local(inputs, gate, filter_taps, cotangent):
    row_count, local_chan = inputs.shape
    block_len = min(128, row_count)
    slot_count = row_count // block_len
    first_block = lax.axis_index("ctx") * slot_count
    seq_total = row_count * lax.axis_size("ctx")
    fwd_cos, fwd_sin, inv_cos, inv_sin = tables(block_len)
    all_taps = lax.all_gather(filter_taps, "ctx", axis=0, tiled=True)
    taps_spec = spectrum(all_taps, block_len, fwd_cos, fwd_sin)
    all_inputs = lax.all_gather(inputs, "ctx", axis=0, tiled=True)
    input_spec = spectrum(all_inputs, block_len, fwd_cos, fwd_sin)
    conv_real, conv_imag = forward_terms(taps_spec, input_spec, first_block, slot_count + 1)
    waves = inverse_many(conv_real, conv_imag, inv_cos, inv_sin)
    convolved = (waves[1:, :block_len] + waves[:-1, block_len:]).reshape(row_count, local_chan)
    gate_wide = gate.astype(jnp.float32)
    upstream = cotangent.astype(jnp.float32)
    mixed = gate_wide * convolved
    squares, projection = lax.psum(
        (jnp.sum(mixed * mixed, axis=1), jnp.sum(upstream * mixed, axis=1)), "chan"
    )
    channels = local_chan * lax.axis_size("chan")
    inv_rms = lax.rsqrt(squares / channels + EPSILON)[:, None]
    output = (mixed * inv_rms).astype(jnp.bfloat16)
    d_mixed = inv_rms * upstream - mixed * inv_rms**3 * projection[:, None] / channels
    gate_grad = (d_mixed * convolved).astype(jnp.bfloat16)
    d_inner = (d_mixed * gate_wide).astype(jnp.bfloat16)
    all_inner = lax.all_gather(d_inner, "ctx", axis=0, tiled=True)
    inner_spec = spectrum(all_inner, block_len, fwd_cos, fwd_sin)
    back_real, back_imag = backward_terms(taps_spec, inner_spec, first_block, slot_count + 1)
    waves = inverse_many(back_real, back_imag, inv_cos, inv_sin)
    input_grad = (
        (waves[:-1, :block_len] + waves[1:, block_len:])
        .reshape(row_count, local_chan)
        .astype(jnp.bfloat16)
    )
    lag_real, lag_imag = owner_terms(input_spec, inner_spec, first_block, slot_count + 1)
    waves = inverse_many(lag_real, lag_imag, inv_cos, inv_sin)
    filter_sum = (waves[:-1, :block_len] + waves[1:, block_len:]).reshape(row_count, local_chan)
    filter_grad = filter_sum / math.sqrt(seq_total)
    return (output, gate_grad, input_grad, filter_grad)


def solution(mesh):
    in_specs = (P("ctx", "chan"), P("ctx", "chan"), P("ctx", "chan"), P("ctx", "chan"))
    out_specs = (P("ctx", "chan"), P("ctx", "chan"), P("ctx", "chan"), P("ctx", "chan"))
    return jax.shard_map(local, mesh=mesh, in_specs=in_specs, out_specs=out_specs, check_vma=False)
```

profile of v0, /device:TPU:1, one launch (start us, length us, event | category | flops | bytes accessed | tf_op | source)
XLA Modules:
  0.0 500.6 jit_solution(9985710225990442809)
XLA Ops:
  10.6 84.2 %all-gather.6.cloned.1.call-done = bf16[2048,256]{1,0:T(8,128)(2,1)} async-done(((bf16[128,256]{1,0:T(8,128)(2,1)}), bf16[2048,256]{1,0:T(8,128)(2,1)}) %all-gather.6.cloned.1.call-update) | async-done | bytes 1048592 | tf_op jit(solution)/shard_map/all_gather | solution.py:116
  94.8 4.0 convolution_bitcast_fusion.1
  98.8 2.6 negate_bitcast_fusion.1
  101.5 65.2 %all-gather.4.cloned.1.call-done = bf16[2048,256]{1,0:T(8,128)(2,1)} async-done(((bf16[128,256]{1,0:T(8,128)(2,1)}), bf16[2048,256]{1,0:T(8,128)(2,1)}) %all-gather.4.cloned.1.call-update) | async-done | bytes 1048592 | tf_op jit(solution)/shard_map/all_gather | solution.py:114
  166.7 2.6 convolution_bitcast_fusion.2
  169.3 2.6 negate_bitcast_fusion.2
  172.0 38.1 %while.63 = (s32[]{:T(128)}, f32[2,129,256]{2,1,0:T(8,128)S(1)}, f32[2,129,256]{2,1,0:T(8,128)S(1)}, f32[16,129,256]{2,1,0:T(8,128)S(1)}, s32[]{:T(128)}, /*inde...) while((s32[]{:T(128)}, f32[2,129,256]{2,1,0:T(8,128)S(1)}, ...), condition=%wide.region_1.2_spmd, body=%wide.region_0.1_spmd.sunk | while | flops 792593 | bytes 2185508 | solution.py:74
  210.1 1.4 fusion.19
  211.5 1.5 fusion.8
  213.0 102.0 %all-reduce = (f32[128]{0:T(128)S(1)}, f32[128]{0:T(128)S(1)}) all-reduce(f32[128]{0:T(128)S(1)} %get-tuple-element.897, f32[128]{0:T(128)S(1)} %get-tuple-element.896), channel_id=1, replica_groups=mesh['chan'=32,'ctx'=16] {'chan'}, use_global_device_ids=true, to_apply=%region_3.4 | all-reduce | flops 256 | bytes 2048 | tf_op jit(solution)/shard_map/psum | solution.py:124
  317.3 84.4 %all-gather.8.cloned.1.call-done = bf16[2048,256]{0,1:T(8,128)(2,1)} async-done(((bf16[128,256]{0,1:T(8,128)(2,1)}), bf16[2048,256]{0,1:T(8,128)(2,1)}) %all-gather.8.cloned.1.call-update) | async-done | bytes 1048592 | tf_op jit(solution)/shard_map/all_gather | solution.py:133
  401.7 1.5 copy.16
  403.2 2.6 convolution_bitcast_fusion
  405.8 2.7 negate_bitcast_fusion
  408.6 40.0 %while.65 = (s32[]{:T(128)}, f32[2,129,256]{2,1,0:T(8,128)S(1)}, f32[2,129,256]{2,1,0:T(8,128)S(1)}, s32[]{:T(128)}, f32[16,129,256]{2,1,0:T(8,128)}, /*index=5*...) while((s32[]{:T(128)}, f32[2,129,256]{2,1,0:T(8,128)S(1)}, ...), condition=%wide.region_9.10_spmd, body=%wide.region_8.9_spmd.sunk | while | flops 792593 | bytes 2171172 | solution.py:104
  409.8 1.2 fusion.131
  414.8 1.2 fusion.131
  417.3 1.2 fusion.131
  419.8 1.2 fusion.131
  448.6 1.4 fusion.15
  450.0 1.5 fusion.6
  452.3 38.1 %while.64 = (s32[]{:T(128)}, f32[2,129,256]{2,1,0:T(8,128)S(1)}, f32[2,129,256]{2,1,0:T(8,128)S(1)}, f32[16,129,256]{2,1,0:T(8,128)S(1)}, s32[]{:T(128)}, /*inde...) while((s32[]{:T(128)}, f32[2,129,256]{2,1,0:T(8,128)S(1)}, ...), condition=%wide.region_7.8_spmd, body=%wide.region_6.7_spmd.sunk | while | flops 792593 | bytes 2185508 | solution.py:89
  490.4 1.4 fusion.17
  491.8 1.5 fusion.7
  (120 shorter events, 116.1 us)
Async XLA Ops:
  7.2 87.7 %all-gather.6.cloned.1.call-start = ((), (), s32[]{:S(2)}) async-start(), calls=%async_computation.1 | async-start | bytes 1114112 | tf_op jit(solution)/shard_map/all_gather | solution.py:116
  7.9 158.8 %all-gather.4.cloned.1.call-start = ((), (), s32[]{:S(2)}) async-start(), calls=%async_computation | async-start | bytes 1114112 | tf_op jit(solution)/shard_map/all_gather | solution.py:114
  8.6 393.1 %all-gather.8.cloned.1.call-start = ((), (), s32[]{:S(2)}) async-start(), calls=%async_computation.2 | async-start | bytes 1114112 | tf_op jit(solution)/shard_map/all_gather | solution.py:133
  94.8 4.0 copy-start
  166.7 2.6 copy-start.1
Sparse Core Ops, SparseCore 0:
  11.3 83.4 all-gather.5
  98.1 68.5 all-gather.3
  315.9 85.7 all-gather.7
where the time goes:
time: 503 us; the launch traced here: 501 us
  waiting for transfers between devices  235 us (47%)
  other arithmetic  114 us (23%)
  blocking collectives  102 us (20%)
  matrix products  25.9 us (5%)
  between operations  13.9 us (3%)
  local copies, waits for them, and re-layouts  6.49 us (1%)
    psum x1, blocking collectives, local(): lax.psum((jnp.sum(mixed * mixed, axis=1), jnp.sum(upstream * mixed, axis=...  102 us
    all_gather x1, waiting for transfers between devices, local(): all_inner = lax.all_gather(d_inner, 'ctx', axis=0, tiled=True)  84.4 us
    all_gather x1, waiting for transfers between devices, local(): all_inputs = lax.all_gather(inputs, 'ctx', axis=0, tiled=True)  84.2 us
    all_gather x1, waiting for transfers between devices, local(): all_taps = lax.all_gather(filter_taps, 'ctx', axis=0, tiled=True)  65.2 us
    scatter-add x32, other arithmetic, owner_advance(): imags = imags.at[target].add(addend[1])  39.1 us
    scatter-add x32, other arithmetic, backward_advance(): imags = imags.at[target].add(addend[1])  37.3 us
    scatter-add x32, other arithmetic, forward_advance(): imags = imags.at[target].add(addend[1])  37.3 us
  transfers between devices with their start and end apart: 3, of which 3 were waited for; matrix products, arithmetic and copies ran while one was open for 2% of the time, Pallas kernels for 0%

commit v1 on v0

--- a/solution.py
+++ b/solution.py
@@ -113,7 +113,13 @@
     fwd_cos, fwd_sin, inv_cos, inv_sin = tables(block_len)
     all_taps = lax.all_gather(filter_taps, "ctx", axis=0, tiled=True)
     taps_spec = spectrum(all_taps, block_len, fwd_cos, fwd_sin)
-    all_inputs = lax.all_gather(inputs, "ctx", axis=0, tiled=True)
+    do_runs = lambda shard_in: jnp.concatenate(
+        lax.all_to_all(
+            jnp.stack([shard_in for _ in range(lax.axis_size("ctx"))], axis=0), "ctx", 0, 0
+        ),
+        axis=0,
+    )
+    all_inputs = do_runs(inputs)
     input_spec = spectrum(all_inputs, block_len, fwd_cos, fwd_sin)
     conv_real, conv_imag = forward_terms(taps_spec, input_spec, first_block, slot_count + 1)
     waves = inverse_many(conv_real, conv_imag, inv_cos, inv_sin)

time: 503 us -> 477 us (0.948)
  waiting for transfers between devices: 235 us -> 191 us
  starting transfers between devices: 0.11 us -> 19.1 us
    all_gather x1 -> x0, waiting for transfers between devices: 84.2 us -> none  [local(): all_inputs = lax.all_gather(inputs, 'ctx', axis=0, tiled=True)]
    all_gather x1, waiting for transfers between devices: 65.2 us -> 106 us  [local(): all_taps = lax.all_gather(filter_taps, 'ctx', axis=0, tiled=True)]
    all_to_all x0 -> x1, starting transfers between devices: none -> 19.1 us  [local(): lax.all_to_all(jnp.stack([shard_in for _ in range(lax.axis_size('ctx'))],...]
  transfers between devices with their start and end apart: 3 -> 3, of which waited for: 3 -> 2; matrix products, arithmetic and copies ran while one was open for 2% -> 1% of each run, Pallas kernels for 0% -> 0%
where the time goes in v1:
time: 477 us; the launch traced here: 475 us
  waiting for transfers between devices  191 us (40%)
  other arithmetic  114 us (24%)
  blocking collectives  102 us (21%)
  matrix products  24.6 us (5%)
  starting transfers between devices  19.1 us (4%)
  between operations  14.2 us (3%)
  local copies, waits for them, and re-layouts  6.76 us (1%)
    all_gather x1, waiting for transfers between devices, local(): all_taps = lax.all_gather(filter_taps, 'ctx', axis=0, tiled=True)  106 us
    psum x1, blocking collectives, local(): lax.psum((jnp.sum(mixed * mixed, axis=1), jnp.sum(upstream * mixed, axis=...  102 us
    all_gather x1, waiting for transfers between devices, local(): all_inner = lax.all_gather(d_inner, 'ctx', axis=0, tiled=True)  84.4 us
    scatter-add x32, other arithmetic, owner_advance(): imags = imags.at[target].add(addend[1])  39.1 us
    scatter-add x32, other arithmetic, forward_advance(): imags = imags.at[target].add(addend[1])  37.3 us
    scatter-add x32, other arithmetic, backward_advance(): imags = imags.at[target].add(addend[1])  37.3 us
    all_to_all x1, starting transfers between devices, local(): lax.all_to_all(jnp.stack([shard_in for _ in range(lax.axis_size('ctx'))],...  19.1 us
  transfers between devices with their start and end apart: 3, of which 2 were waited for; matrix products, arithmetic and copies ran while one was open for 1% of the time, Pallas kernels for 0%

profile of v1, /device:TPU:1, one launch (start us, length us, event | category | flops | bytes accessed | tf_op | source)
XLA Modules:
  0.0 475.1 jit_solution(2738865523812884529)
XLA Ops:
  7.2 2.0 stack.2
  9.1 19.1 %all-to-all-start = ((bf16[16,128,256]{2,1,0:T(8,128)(2,1)}), bf16[16,128,256]{2,1,0:T(8,128)(2,1)S(1)}, u32[]{:S(2)}, u32[]{:S(2)}) async-start(bf16[16,128,256]{2,1,0:T(8,128)(2,1)} %stack.2), calls=%async_computation | async-start | bytes 2097152 | tf_op jit(solution)/shard_map/all_to_all | solution.py:117
  29.3 106.3 %all-gather.3.cloned.1.call-done = bf16[2048,256]{1,0:T(8,128)(2,1)} async-done(((bf16[128,256]{1,0:T(8,128)(2,1)}), bf16[2048,256]{1,0:T(8,128)(2,1)}) %all-gather.3.cloned.1.call-update) | async-done | bytes 1048592 | tf_op jit(solution)/shard_map/all_gather | solution.py:114
  135.5 2.6 convolution_bitcast_fusion.2
  138.1 2.6 negate_bitcast_fusion.2
  140.7 2.7 convolution_bitcast_fusion.1
  143.5 2.6 negate_bitcast_fusion.1
  146.1 38.1 %while.63 = (s32[]{:T(128)}, f32[2,129,256]{2,1,0:T(8,128)S(1)}, f32[2,129,256]{2,1,0:T(8,128)S(1)}, f32[16,129,256]{2,1,0:T(8,128)S(1)}, s32[]{:T(128)}, /*inde...) while((s32[]{:T(128)}, f32[2,129,256]{2,1,0:T(8,128)S(1)}, ...), condition=%wide.region_1.2_spmd, body=%wide.region_0.1_spmd.sunk | while | flops 792593 | bytes 2185508 | solution.py:74
  184.2 1.4 fusion.19
  185.7 1.5 fusion.8
  187.2 102.0 %all-reduce = (f32[128]{0:T(128)S(1)}, f32[128]{0:T(128)S(1)}) all-reduce(f32[128]{0:T(128)S(1)} %get-tuple-element.897, f32[128]{0:T(128)S(1)} %get-tuple-element.896), channel_id=1, replica_groups=mesh['chan'=32,'ctx'=16] {'chan'}, use_global_device_ids=true, to_apply=%region_3.4 | all-reduce | flops 256 | bytes 2048 | tf_op jit(solution)/shard_map/psum | solution.py:130
  291.4 84.4 %all-gather.5.cloned.1.call-done = bf16[2048,256]{0,1:T(8,128)(2,1)} async-done(((bf16[128,256]{0,1:T(8,128)(2,1)}), bf16[2048,256]{0,1:T(8,128)(2,1)}) %all-gather.5.cloned.1.call-update) | async-done | bytes 1048592 | tf_op jit(solution)/shard_map/all_gather | solution.py:139
  375.9 1.5 copy.16
  377.4 2.6 convolution_bitcast_fusion
  380.0 2.7 negate_bitcast_fusion
  382.7 40.0 %while.65 = (s32[]{:T(128)}, f32[2,129,256]{2,1,0:T(8,128)S(1)}, f32[2,129,256]{2,1,0:T(8,128)S(1)}, s32[]{:T(128)}, f32[16,129,256]{2,1,0:T(8,128)}, /*index=5*...) while((s32[]{:T(128)}, f32[2,129,256]{2,1,0:T(8,128)S(1)}, ...), condition=%wide.region_9.10_spmd, body=%wide.region_8.9_spmd.sunk | while | flops 792593 | bytes 2171172 | solution.py:104
  384.0 1.2 fusion.131
  386.5 1.2 fusion.131
  389.0 1.2 fusion.131
  422.7 1.4 fusion.15
  424.2 1.5 fusion.6
  426.5 38.1 %while.64 = (s32[]{:T(128)}, f32[2,129,256]{2,1,0:T(8,128)S(1)}, f32[2,129,256]{2,1,0:T(8,128)S(1)}, f32[16,129,256]{2,1,0:T(8,128)S(1)}, s32[]{:T(128)}, /*inde...) while((s32[]{:T(128)}, f32[2,129,256]{2,1,0:T(8,128)S(1)}, ...), condition=%wide.region_7.8_spmd, body=%wide.region_6.7_spmd.sunk | while | flops 792593 | bytes 2185508 | solution.py:89
  464.6 1.4 fusion.17
  466.0 1.5 fusion.7
  (122 shorter events, 114.9 us)
Async XLA Ops:
  7.2 21.8 %copy-start.1 = (bf16[128,256]{1,0:T(8,128)(2,1)S(1)}, bf16[128,256]{1,0:T(8,128)(2,1)}, u32[]{:S(2)}) copy-start(bf16[128,256]{1,0:T(8,128)(2,1)} %param.35) | copy-start | bytes 196612
  7.2 21.9 %copy-start.2 = (bf16[128,256]{1,0:T(8,128)(2,1)S(1)}, bf16[128,256]{1,0:T(8,128)(2,1)}, u32[]{:S(2)}) copy-start(bf16[128,256]{1,0:T(8,128)(2,1)} %param.37) | copy-start | bytes 196612
  9.1 131.6 %all-to-all-start = ((bf16[16,128,256]{2,1,0:T(8,128)(2,1)}), bf16[16,128,256]{2,1,0:T(8,128)(2,1)S(1)}, u32[]{:S(2)}, u32[]{:S(2)}) async-start(bf16[16,128,256]{2,1,0:T(8,128)(2,1)} %stack.2), calls=%async_computation | async-start | bytes 2097152 | tf_op jit(solution)/shard_map/all_to_all | solution.py:117
  28.2 107.3 %all-gather.3.cloned.1.call-start = ((), (), s32[]{:S(2)}) async-start(), calls=%async_computation.1 | async-start | bytes 1114112 | tf_op jit(solution)/shard_map/all_gather | solution.py:114
  28.9 347.0 %all-gather.5.cloned.1.call-start = ((), (), s32[]{:S(2)}) async-start(), calls=%async_computation.2 | async-start | bytes 1114112 | tf_op jit(solution)/shard_map/all_gather | solution.py:139
  135.5 2.6 copy-start
Sparse Core Ops, SparseCore 0:
  32.4 103.1 all-gather.2
  290.1 85.7 all-gather.4
